TPU v7x, 32 devices: a whole 2x2x4 slice. The times are simulated.
32 devices in a mesh: tm: 4 (over y, x), space: 8 (over z, core).
Axes of the slice: x: 2, y: 2, z: 4, core: 2. Of those that a mesh axis runs over, the one named last changes fastest.
Arguments:
- queries: bfloat16 [4, 768, 3072], P('tm', 'space'), may hold values from -8 to 8
- key_rows: bfloat16 [4, 768, 3072], P('tm', 'space'), may hold values from -8 to 8
- value_rows: bfloat16 [4, 768, 3072], P('tm', 'space'), may hold values from -6 to 6
- noise_level: int32 [4], P('tm'), may hold values from 0 to 999
- decay_power: int32 [24], replicated, may hold values from 0 to 7
- head_gain: float32 [24, 128], replicated, may hold values from 0.1 to 1.9
Outputs:
- attended: bfloat16 [4, 768, 3072], P('tm', 'space')
All inputs are finite; a program needn't handle non-finite values.
Results may differ from a plain program's by a relative error of at most 0.0049.
Values may be sent and summed in bfloat16 or wider, within the bound.
A program may use at most 64 MiB of HBM per device.

v0:
```python
import jax
import jax.numpy as jnp
from jax import lax
from jax.sharding import PartitionSpec as P

LEVELS = 1000
HGROUPS = 8
epsilon = 1e-06


def carried_in(value, axis, join, neutral):
    count, mine = (lax.axis_size(axis), lax.axis_index(axis))
    pieces = jax.tree.map(lambda part: lax.all_gather(part, axis), value)
    so_far = jax.tree.map(
        lambda part, zero: jnp.full_like(part, 0) + jnp.asarray(zero, part.dtype), value, neutral
    )

    def lap(position, so_far):
        longer = join(so_far, jax.tree.map(lambda part: part[position], pieces))
        return jax.tree.map(lambda new, old: jnp.where(position < mine, new, old), longer, so_far)

    return lax.fori_loop(0, count - 1, lap, so_far)


def spread_items(block, quarters, heads_total, depth):
    part_rows = block.shape[0] // quarters
    shaped = block.reshape(quarters, part_rows, heads_total, depth).transpose(0, 2, 1, 3)
    return shaped.reshape(quarters * heads_total, part_rows, depth)


def copied_items(block, quarters, heads_total, depth):
    every = block.reshape(block.shape[0], heads_total, depth).transpose(1, 0, 2)
    copied = jnp.broadcast_to(every[None], (quarters,) + every.shape)
    return copied.reshape(quarters * heads_total, block.shape[0], depth)


def attend_head(bundle):
    query, key_item, value_item, state, gain_row = bundle
    factor = query.shape[1] ** (-0.5)
    scores = jnp.dot(query, key_item.T, preferred_element_type=jnp.float32) * factor
    row_top = jnp.max(scores, axis=1, keepdims=True)
    weights = jnp.exp(scores - row_top)
    row_total = jnp.sum(weights, axis=1, keepdims=True)
    numerator = jnp.dot(
        weights.astype(jnp.bfloat16), value_item, preferred_element_type=jnp.float32
    )
    carried = jnp.dot(query, state, preferred_element_type=jnp.float32) * factor
    mixed = numerator / row_total + carried
    normed = mixed * lax.rsqrt(jnp.mean(mixed * mixed, axis=1, keepdims=True) + epsilon) * gain_row
    return normed.astype(jnp.bfloat16)


def compose(earlier, later):
    return (earlier[0] * later[0], later[0][:, None, None] * earlier[1] + later[1])


def body(queries, key_rows, value_rows, noise_level, decay_power, head_gain):
    heads_total = decay_power.shape[0]
    depth = head_gain.shape[1]
    local_rows = queries.shape[1]
    quarters = lax.axis_size("space") // HGROUPS
    grouped = heads_total // HGROUPS
    query_items = spread_items(queries[0], quarters, heads_total, depth)
    keys_sent = copied_items(key_rows[0], quarters, heads_total, depth)
    values_sent = copied_items(value_rows[0], quarters, heads_total, depth)
    query_got, keys_got, values_got = (
        lax.all_to_all(query_items, "space", split_axis=0, concat_axis=1, tiled=True),
        lax.all_to_all(keys_sent, "space", split_axis=0, concat_axis=1, tiled=True),
        lax.all_to_all(values_sent, "space", split_axis=0, concat_axis=1, tiled=True),
    )
    key_count = keys_got.shape[1]
    fresh = (
        jnp.einsum("inh,ine->ihe", keys_got, values_got, preferred_element_type=jnp.float32)
        / key_count
    )
    group_index = lax.axis_index("space") % HGROUPS
    powers = lax.dynamic_slice_in_dim(decay_power, group_index * grouped, grouped).astype(
        jnp.float32
    )
    level_now = noise_level[0].astype(jnp.float32)
    block_count = lax.axis_size("tm")
    rate = jnp.exp2(-(powers * (0.25 + 1.75 * level_now / LEVELS)) / block_count)
    zeros_state = jnp.zeros_like(fresh)
    unused_rate, before = carried_in(
        (rate, fresh), "tm", compose, (jnp.ones_like(rate), zeros_state)
    )
    state = (rate[:, None, None] * before).astype(jnp.bfloat16)
    gain_rows = lax.dynamic_slice_in_dim(head_gain, group_index * grouped, grouped)
    outcome = lax.map(attend_head, (query_got, keys_got, values_got, state, gain_rows))
    returned = lax.all_to_all(outcome, "space", split_axis=1, concat_axis=0, tiled=True)
    part_rows = local_rows // quarters
    restored = returned.reshape(quarters, heads_total, part_rows, depth).transpose(0, 2, 1, 3)
    return restored.reshape(1, local_rows, heads_total * depth)


def solution(mesh):
    in_specs = (
        P("tm", "space", None),
        P("tm", "space", None),
        P("tm", "space", None),
        P("tm"),
        P(),
        P(),
    )
    out_specs = P("tm", "space", None)
    return jax.shard_map(body, mesh=mesh, in_specs=in_specs, out_specs=out_specs, check_vma=False)
```

profile of v0, /device:TPU:0, one launch (start us, length us, event | category | flops | bytes accessed | tf_op | source)
XLA Modules:
  0.0 99.5 jit_solution(8693053812802755996)
XLA Ops:
  0.0 0.0 copy-start
  0.0 0.0 copy-start.1
  0.0 1.2 %copy.38 = bf16[12,8,24,128]{3,2,1,0:T(8,128)(2,1)S(1)} copy(bf16[12,8,24,128]{3,1,2,0:T(8,128)(2,1)} %bitcast.111) | data formatting | bytes 1179648
  1.2 0.9 copy.26
  2.1 0.0 copy-start.4
  2.1 0.0 copy-start.3
  2.2 0.0 copy-start.2
  2.2 6.5 %all-to-all-start.1 = ((bf16[24,96,128]{2,1,0:T(8,128)(2,1)}), bf16[24,96,128]{2,1,0:T(8,128)(2,1)S(1)}, u32[]{:S(2)}, u32[]{:S(2)}) async-start(bf16[24,96,128]{2,1,0:T(8,128)(2,1)} %copy.26), calls=%async_computation.1 | async-start | bytes 1179648 | tf_op jit(solution)/shard_map/all_to_all | solution.py:68
  8.6 0.0 copy-done.1
  8.6 0.1 copy.39
  8.8 0.9 copy.28
  9.7 15.7 %all-to-all-done.1 = bf16[24,96,128]{2,1,0:T(8,128)(2,1)S(1)} async-done(((bf16[24,96,128]{2,1,0:T(8,128)(2,1)}), bf16[24,96,128]{2,1,0:T(8,128)(2,1)S(1)}, u32[]{:S(2)}, u32[]{:S(2)}) %all-to-all-start.1) | async-done | bytes 589856 | tf_op jit(solution)/shard_map/all_to_all | solution.py:68
  25.4 3.5 %all-to-all-start.2 = ((bf16[24,96,128]{2,1,0:T(8,128)(2,1)}), bf16[24,96,128]{2,1,0:T(8,128)(2,1)S(1)}, u32[]{:S(2)}, u32[]{:S(2)}) async-start(bf16[24,96,128]{2,1,0:T(8,128)(2,1)} %copy.28), calls=%async_computation.2 | async-start | bytes 1179648 | tf_op jit(solution)/shard_map/all_to_all | solution.py:69
  29.6 0.0 copy-done.4
  29.6 0.6 dynamic-slice
  30.9 0.0 copy-done.3
  30.9 0.2 fusion.25
  31.0 9.9 %all-reduce = f32[12]{0:T(128)S(1)} all-reduce(f32[12]{0:T(128)S(1)} %get-tuple-element.187), channel_id=2, replica_groups=mesh['tm'=4,'space'=8] {'tm'}, use_global_device_ids=true, to_apply=%add | all-reduce | flops 12 | bytes 96
  40.9 0.1 reshape.30
  41.0 0.0 copy-done.2
  41.0 0.1 copy.37
  41.1 0.1 bitcast_bitcast_fusion
  41.2 0.9 copy.24
  42.1 0.0 copy-done
  42.2 3.4 %all-to-all-done.2 = bf16[24,96,128]{2,1,0:T(8,128)(2,1)S(1)} async-done(((bf16[24,96,128]{2,1,0:T(8,128)(2,1)}), bf16[24,96,128]{2,1,0:T(8,128)(2,1)S(1)}, u32[]{:S(2)}, u32[]{:S(2)}) %all-to-all-start.2) | async-done | bytes 589856 | tf_op jit(solution)/shard_map/all_to_all | solution.py:69
  45.6 3.5 %all-to-all-start = ((bf16[24,96,128]{2,1,0:T(8,128)(2,1)}), bf16[24,96,128]{2,1,0:T(8,128)(2,1)S(1)}, u32[]{:S(2)}, u32[]{:S(2)}) async-start(bf16[24,96,128]{2,1,0:T(8,128)(2,1)} %copy.24), calls=%async_computation | async-start | bytes 1179648 | tf_op jit(solution)/shard_map/all_to_all | solution.py:67
  49.2 0.4 convolution_multiply_fusion.1
  49.5 12.5 %all-gather.1 = f32[12,128,128]{2,1,0:T(8,128)S(1)} all-gather(f32[3,128,128]{2,1,0:T(8,128)S(1)} %convolution_multiply_fusion.1), channel_id=3, replica_groups=mesh['tm'=4,'space'=8] {'tm'}, dimensions={0}, use_global_device_ids=true | all-gather | bytes 983040 | tf_op jit(solution)/shard_map/all_gather | solution.py:13
  62.1 0.4 while.25
  62.1 0.1 fusion.39
  62.2 0.1 fusion.39
  62.4 0.1 fusion.39
  62.5 3.3 %all-to-all-done = bf16[24,96,128]{2,1,0:T(8,128)(2,1)S(1)} async-done(((bf16[24,96,128]{2,1,0:T(8,128)(2,1)}), bf16[24,96,128]{2,1,0:T(8,128)(2,1)S(1)}, u32[]{:S(2)}, u32[]{:S(2)}) %all-to-all-start) | async-done | bytes 589856 | tf_op jit(solution)/shard_map/all_to_all | solution.py:67
  65.8 0.1 multiply_convert_fusion.1
  65.9 7.7 %while.24 = (s32[]{:T(128)}, bf16[3,768,128]{1,2,0:T(8,128)(2,1)}, bf16[3,768,128]{2,1,0:T(8,128)(2,1)S(1)}, bf16[3,768,128]{2,1,0:T(8,128)(2,1)S(1)}, bf16[3,76...) while((s32[]{:T(128)}, bf16[3,768,128]{1,2,0:T(8,128)(2,1)}, ...), condition=%wide.region_6.7_spmd, body=%wide.region_2.6_spmd.sunk | while | flops 332659968 | bytes 9700445 | solution.py:89
  65.9 0.5 multiply_reduce_fusion.4
  66.4 0.4 fusion.36
  66.8 0.2 convolution_multiply_fusion.3
  67.1 0.6 multiply_reduce_fusion.5
  67.7 0.8 fusion.38
  68.5 0.5 multiply_reduce_fusion.4
  69.0 0.4 fusion.36
  69.4 0.3 convolution_multiply_fusion.3
  69.7 0.6 multiply_reduce_fusion.5
  70.3 0.8 fusion.38
  71.0 0.5 multiply_reduce_fusion.4
  71.5 0.4 fusion.36
  71.9 0.3 convolution_multiply_fusion.3
  72.2 0.6 multiply_reduce_fusion.5
  72.8 0.8 fusion.38
  73.6 1.5 %copy.31 = bf16[3,768,128]{2,0,1:T(4,128)(2,1)S(1)} copy(bf16[3,768,128]{1,2,0:T(8,128)(2,1)} %get-tuple-element.137) | data formatting | bytes 1179648 | tf_op jit(solution)/shard_map/while | solution.py:89
  75.1 23.4 %all_to_all.69 = bf16[3,768,128]{2,0,1:T(4,128)(2,1)S(1)} all-to-all(bf16[3,768,128]{2,0,1:T(4,128)(2,1)S(1)} %copy.31), channel_id=1, replica_groups=mesh['tm'=4,'space'=8] {'space'}, dimensions={1} | all-to-all | bytes 1179648 | tf_op jit(solution)/shard_map/all_to_all | solution.py:90
  98.4 0.1 copy.32
  98.6 1.0 copy.41
  (17 shorter events, 0.3 us)
Async XLA Ops:
  0.0 42.1 %copy-start = (f32[24,128]{1,0:T(8,128)S(1)}, f32[24,128]{1,0:T(8,128)}, u32[]{:S(2)}) copy-start(f32[24,128]{1,0:T(8,128)} %param.15) | copy-start | bytes 36868
  0.0 8.6 %copy-start.1 = (bf16[1,96,3072]{2,1,0:T(8,128)(2,1)S(1)}, bf16[1,96,3072]{2,1,0:T(8,128)(2,1)}, u32[]{:S(2)}) copy-start(bf16[1,96,3072]{2,1,0:T(8,128)(2,1)} %param.12) | copy-start | bytes 1769476
  2.1 27.4 %copy-start.4 = (u32[32]{0:T(128)S(1)}, u32[32]{0:T(128)}, u32[]{:S(2)}) copy-start(u32[32]{0:T(128)} %constant.102) | copy-start | bytes 388
  2.1 28.7 %copy-start.3 = (s32[24]{0:T(128)S(1)}, s32[24]{0:T(128)}, u32[]{:S(2)}) copy-start(s32[24]{0:T(128)} %param.14) | copy-start | bytes 292
  2.2 38.9 %copy-start.2 = (bf16[1,96,3072]{2,1,0:T(8,128)(2,1)S(1)}, bf16[1,96,3072]{2,1,0:T(8,128)(2,1)}, u32[]{:S(2)}) copy-start(bf16[1,96,3072]{2,1,0:T(8,128)(2,1)} %param.10) | copy-start | bytes 1769476
  2.2 23.2 %all-to-all-start.1 = ((bf16[24,96,128]{2,1,0:T(8,128)(2,1)}), bf16[24,96,128]{2,1,0:T(8,128)(2,1)S(1)}, u32[]{:S(2)}, u32[]{:S(2)}) async-start(bf16[24,96,128]{2,1,0:T(8,128)(2,1)} %copy.26), calls=%async_computation.1 | async-start | bytes 1179648 | tf_op jit(solution)/shard_map/all_to_all | solution.py:68
  25.4 20.2 %all-to-all-start.2 = ((bf16[24,96,128]{2,1,0:T(8,128)(2,1)}), bf16[24,96,128]{2,1,0:T(8,128)(2,1)S(1)}, u32[]{:S(2)}, u32[]{:S(2)}) async-start(bf16[24,96,128]{2,1,0:T(8,128)(2,1)} %copy.28), calls=%async_computation.2 | async-start | bytes 1179648 | tf_op jit(solution)/shard_map/all_to_all | solution.py:69
  45.6 20.2 %all-to-all-start = ((bf16[24,96,128]{2,1,0:T(8,128)(2,1)}), bf16[24,96,128]{2,1,0:T(8,128)(2,1)S(1)}, u32[]{:S(2)}, u32[]{:S(2)}) async-start(bf16[24,96,128]{2,1,0:T(8,128)(2,1)} %copy.24), calls=%async_computation | async-start | bytes 1179648 | tf_op jit(solution)/shard_map/all_to_all | solution.py:67
where the time goes:
time: 100 us; the launch traced here: 99.5 us
  blocking collectives  45.8 us (46%)
  waiting for transfers between devices  22.4 us (22%)
  starting transfers between devices  13.6 us (14%)
  local copies, waits for them, and re-layouts  7.68 us (8%)
  matrix products  4.3 us (4%)
  other arithmetic  4.18 us (4%)
  between operations  1.48 us (1%)
    all_to_all x1, blocking collectives, body(): lax.all_to_all(outcome, 'space', split_axis=1, concat_axis=0, tiled=True)  23.4 us
    all_to_all x1, waiting for transfers between devices, body(): lax.all_to_all(keys_sent, 'space', split_axis=0, concat_axis=1, tiled=True)  15.7 us
    all_gather x1, blocking collectives, carried_in(): pieces = jax.tree.map(lambda part: lax.all_gather(part, axis), value)  12.5 us
    unnamed x1, blocking collectives  9.88 us
    all_to_all x1, starting transfers between devices, body(): lax.all_to_all(keys_sent, 'space', split_axis=0, concat_axis=1, tiled=True)  6.49 us
    all_to_all x1, starting transfers between devices, body(): lax.all_to_all(values_sent, 'space', split_axis=0, concat_axis=1, tiled=T...  3.54 us
    all_to_all x1, starting transfers between devices, body(): lax.all_to_all(query_items, 'space', split_axis=0, concat_axis=1, tiled=T...  3.54 us
    all_to_all x1, waiting for transfers between devices, body(): lax.all_to_all(values_sent, 'space', split_axis=0, concat_axis=1, tiled=T...  3.4 us
  transfers between devices with their start and end apart: 3, of which 3 were waited for; matrix products, arithmetic and copies ran while one was open for 4% of the time, Pallas kernels for 0%

commit v1 on v0

--- a/solution.py
+++ b/solution.py
@@ -6,6 +6,29 @@
 LEVELS = 1000
 HGROUPS = 8
 epsilon = 1e-06
+
+
+def split_up(x, dim, size):
+    lengths = x.shape
+    blocks = x.reshape(*lengths[:dim], size, lengths[dim] // size, *lengths[dim + 1 :])
+    return jnp.moveaxis(blocks, dim, 0)
+
+
+def in_order(blocks, dim):
+    shape = list(blocks.shape[1:])
+    shape[dim] *= blocks.shape[0]
+    return jnp.moveaxis(blocks, 0, dim).reshape(shape)
+
+
+def swapped_with_each(value, axis, split_dim, concat_dim):
+    size, index = (lax.axis_size(axis), lax.axis_index(axis))
+    blocks = split_up(value, split_dim, size)
+    outs = [blocks[index]]
+    for turn in range(1, size):
+        sent = blocks[index ^ turn]
+        outs.append(lax.ppermute(sent, axis, [(i, i ^ turn) for i in range(size)]))
+    blocks = jnp.stack(outs)[index ^ jnp.arange(size)]
+    return in_order(blocks, concat_dim)
 
 
 def carried_in(value, axis, join, neutral):
@@ -87,7 +110,7 @@
     state = (rate[:, None, None] * before).astype(jnp.bfloat16)
     gain_rows = lax.dynamic_slice_in_dim(head_gain, group_index * grouped, grouped)
     outcome = lax.map(attend_head, (query_got, keys_got, values_got, state, gain_rows))
-    returned = lax.all_to_all(outcome, "space", split_axis=1, concat_axis=0, tiled=True)
+    returned = swapped_with_each(outcome, "space", 1, 0)
     part_rows = local_rows // quarters
     restored = returned.reshape(quarters, heads_total, part_rows, depth).transpose(0, 2, 1, 3)
     return restored.reshape(1, local_rows, heads_total * depth)

time: 100 us -> 93.3 us (0.933); the launches traced: 99.5 us -> 91.8 us
  blocking collectives: 45.8 us -> 22.4 us
  starting transfers between devices: 13.6 us -> 21.8 us
  waiting for transfers between devices: 22.4 us -> 28 us
  local copies, waits for them, and re-layouts: 7.68 us -> 11.4 us
  other arithmetic: 4.18 us -> 2.14 us
    all_to_all x1 -> x0, blocking collectives: 23.4 us -> none  [body(): lax.all_to_all(outcome, 'space', split_axis=1, concat_axis=0, tiled=True)]
    ppermute x0 -> x7, starting transfers between devices: none -> 8.23 us  [swapped_with_each(): outs.append(lax.ppermute(sent, axis, [(i, i ^ turn) for i in range(size)]))]
    ppermute x0 -> x7, waiting for transfers between devices: none -> 5.65 us  [swapped_with_each(): outs.append(lax.ppermute(sent, axis, [(i, i ^ turn) for i in range(size)]))]
    dynamic_update_slice x0 -> x6, local copies, waits for them, and re-layouts: none -> 2.57 us  [body(): lax.map(attend_head, (query_got, keys_got, values_got, state, gain_rows))]
    dynamic_update_slice x3 -> x0, other arithmetic: 2.32 us -> none  [body(): lax.map(attend_head, (query_got, keys_got, values_got, state, gain_rows))]
    while x1 -> x0, local copies, waits for them, and re-layouts: 1.47 us -> none  [body(): lax.map(attend_head, (query_got, keys_got, values_got, state, gain_rows))]
    squeeze x0 -> x1, local copies, waits for them, and re-layouts: none -> 1.14 us  [swapped_with_each(): sent = blocks[index ^ turn]]
    unnamed x15 -> x22, local copies, waits for them, and re-layouts: 2.04 us -> 3.02 us
  transfers between devices with their start and end apart: 3 -> 10, of which waited for: 3 -> 5; matrix products, arithmetic and copies ran while one was open for 4% -> 5% of each run, Pallas kernels for 0% -> 0%
where the time goes in v1:
time: 93.3 us; the launch traced here: 91.8 us
  waiting for transfers between devices  28 us (30%)
  blocking collectives  22.4 us (24%)
  starting transfers between devices  21.8 us (23%)
  local copies, waits for them, and re-layouts  11.4 us (12%)
  matrix products  4.28 us (5%)
  other arithmetic  2.14 us (2%)
  between operations  1.57 us (2%)
    all_to_all x1, waiting for transfers between devices, body(): lax.all_to_all(keys_sent, 'space', split_axis=0, concat_axis=1, tiled=True)  15.7 us
    all_gather x1, blocking collectives, carried_in(): pieces = jax.tree.map(lambda part: lax.all_gather(part, axis), value)  12.5 us
    unnamed x1, blocking collectives  9.88 us
    ppermute x7, starting transfers between devices, swapped_with_each(): outs.append(lax.ppermute(sent, axis, [(i, i ^ turn) for i in range(size)]))  8.23 us
    all_to_all x1, starting transfers between devices, body(): lax.all_to_all(keys_sent, 'space', split_axis=0, concat_axis=1, tiled=True)  6.49 us
    ppermute x7, waiting for transfers between devices, swapped_with_each(): outs.append(lax.ppermute(sent, axis, [(i, i ^ turn) for i in range(size)]))  5.65 us
    all_to_all x1, starting transfers between devices, body(): lax.all_to_all(values_sent, 'space', split_axis=0, concat_axis=1, tiled=T...  3.54 us
    all_to_all x1, starting transfers between devices, body(): lax.all_to_all(query_items, 'space', split_axis=0, concat_axis=1, tiled=T...  3.54 us
  transfers between devices with their start and end apart: 10, of which 5 were waited for; matrix products, arithmetic and copies ran while one was open for 5% of the time, Pallas kernels for 0%

profile of v1, /device:TPU:0, one launch (start us, length us, event | category | flops | bytes accessed | tf_op | source)
XLA Modules:
  0.0 91.8 jit_solution(7260103150056672376)
XLA Ops:
  0.0 1.2 %copy.35 = bf16[12,8,24,128]{3,2,1,0:T(8,128)(2,1)S(1)} copy(bf16[12,8,24,128]{3,1,2,0:T(8,128)(2,1)} %bitcast.138) | data formatting | bytes 1179648
  1.2 0.9 copy.23
  2.2 6.5 %all-to-all-start.1 = ((bf16[24,96,128]{2,1,0:T(8,128)(2,1)}), bf16[24,96,128]{2,1,0:T(8,128)(2,1)S(1)}, u32[]{:S(2)}, u32[]{:S(2)}) async-start(bf16[24,96,128]{2,1,0:T(8,128)(2,1)} %copy.23), calls=%async_computation.1 | async-start | bytes 1179648 | tf_op jit(solution)/shard_map/all_to_all | solution.py:91
  8.6 0.1 copy.36
  8.8 0.9 copy.25
  9.7 15.7 %all-to-all-done.1 = bf16[24,96,128]{2,1,0:T(8,128)(2,1)S(1)} async-done(((bf16[24,96,128]{2,1,0:T(8,128)(2,1)}), bf16[24,96,128]{2,1,0:T(8,128)(2,1)S(1)}, u32[]{:S(2)}, u32[]{:S(2)}) %all-to-all-start.1) | async-done | bytes 589856 | tf_op jit(solution)/shard_map/all_to_all | solution.py:91
  25.4 3.5 %all-to-all-start.2 = ((bf16[24,96,128]{2,1,0:T(8,128)(2,1)}), bf16[24,96,128]{2,1,0:T(8,128)(2,1)S(1)}, u32[]{:S(2)}, u32[]{:S(2)}) async-start(bf16[24,96,128]{2,1,0:T(8,128)(2,1)} %copy.25), calls=%async_computation.2 | async-start | bytes 1179648 | tf_op jit(solution)/shard_map/all_to_all | solution.py:92
  29.6 0.6 dynamic-slice.32
  30.9 0.2 fusion.25
  31.0 9.9 %all-reduce = f32[12]{0:T(128)S(1)} all-reduce(f32[12]{0:T(128)S(1)} %get-tuple-element.187), channel_id=2, replica_groups=mesh['tm'=4,'space'=8] {'tm'}, use_global_device_ids=true, to_apply=%add | all-reduce | flops 12 | bytes 96
  41.0 0.1 reshape.68
  41.0 0.1 copy.34
  41.2 0.1 bitcast_bitcast_fusion
  41.2 0.9 copy.21
  42.2 3.4 %all-to-all-done.2 = bf16[24,96,128]{2,1,0:T(8,128)(2,1)S(1)} async-done(((bf16[24,96,128]{2,1,0:T(8,128)(2,1)}), bf16[24,96,128]{2,1,0:T(8,128)(2,1)S(1)}, u32[]{:S(2)}, u32[]{:S(2)}) %all-to-all-start.2) | async-done | bytes 589856 | tf_op jit(solution)/shard_map/all_to_all | solution.py:92
  45.6 3.5 %all-to-all-start = ((bf16[24,96,128]{2,1,0:T(8,128)(2,1)}), bf16[24,96,128]{2,1,0:T(8,128)(2,1)S(1)}, u32[]{:S(2)}, u32[]{:S(2)}) async-start(bf16[24,96,128]{2,1,0:T(8,128)(2,1)} %copy.21), calls=%async_computation | async-start | bytes 1179648 | tf_op jit(solution)/shard_map/all_to_all | solution.py:90
  49.2 0.4 convolution_multiply_fusion.1
  49.5 12.5 %all-gather.1 = f32[12,128,128]{2,1,0:T(8,128)S(1)} all-gather(f32[3,128,128]{2,1,0:T(8,128)S(1)} %convolution_multiply_fusion.1), channel_id=3, replica_groups=mesh['tm'=4,'space'=8] {'tm'}, dimensions={0}, use_global_device_ids=true | all-gather | bytes 983040 | tf_op jit(solution)/shard_map/all_gather | solution.py:36
  62.1 0.4 while.25
  62.1 0.1 fusion.39
  62.2 0.1 fusion.39
  62.4 0.1 fusion.39
  62.5 3.3 %all-to-all-done = bf16[24,96,128]{2,1,0:T(8,128)(2,1)S(1)} async-done(((bf16[24,96,128]{2,1,0:T(8,128)(2,1)}), bf16[24,96,128]{2,1,0:T(8,128)(2,1)S(1)}, u32[]{:S(2)}, u32[]{:S(2)}) %all-to-all-start) | async-done | bytes 589856 | tf_op jit(solution)/shard_map/all_to_all | solution.py:90
  65.8 0.1 multiply_convert_fusion.1
  65.9 8.2 %while.24 = (s32[]{:T(128)}, bf16[3,768,128]{2,1,0:T(8,128)(2,1)}, bf16[3,768,128]{2,1,0:T(8,128)(2,1)S(1)}, bf16[3,768,128]{2,1,0:T(8,128)(2,1)S(1)}, bf16[3,76...) while((s32[]{:T(128)}, bf16[3,768,128]{2,1,0:T(8,128)(2,1)}, ...), condition=%wide.region_6.7_spmd, body=%wide.region_2.6_spmd.sunk | while | flops 332659968 | bytes 10486877 | solution.py:112
  65.9 0.5 multiply_reduce_fusion.4
  66.4 0.4 fusion.36
  66.8 0.2 convolution_multiply_fusion.3
  67.1 0.6 multiply_reduce_fusion.5
  67.7 0.1 fusion.38
  67.8 0.2 copy.40
  68.0 0.7 constant_dynamic-update-slice_fusion.2
  68.7 0.5 multiply_reduce_fusion.4
  69.1 0.4 fusion.36
  69.6 0.3 convolution_multiply_fusion.3
  69.8 0.6 multiply_reduce_fusion.5
  70.4 0.1 fusion.38
  70.5 0.2 copy.40
  70.7 0.7 constant_dynamic-update-slice_fusion.2
  71.4 0.5 multiply_reduce_fusion.4
  71.9 0.4 fusion.36
  72.3 0.2 convolution_multiply_fusion.3
  72.6 0.6 multiply_reduce_fusion.5
  73.2 0.1 fusion.38
  73.3 0.2 copy.40
  73.4 0.7 constant_dynamic-update-slice_fusion.2
  74.1 1.1 %dynamic-slice_bitcast_fusion.1 = (bf16[3,96,128]{2,1,0:T(8,128)(2,1)S(1)}, bf16[3,96,128]{2,1,0:T(8,128)(2,1)S(1)}, bf16[3,96,128]{2,1,0:T(8,128)(2,1)S(1)}, bf...) fusion(bf16[3,8,96,128]{3,2,1,0:T(8,128)(2,1)} %bitcast.141, ...), kind=kLoop, calls=%fused_computation.47 | loop fusion | bytes 1032220 | tf_op jit(solution)/shard_map/squeeze | solution.py:28
  75.3 0.1 collective-permute-start
  75.3 0.1 collective-permute-start.1
  75.4 1.8 %collective-permute-start.2 = (bf16[3,96,128]{2,1,0:T(8,128)(2,1)S(1)}, bf16[3,96,128]{2,1,0:T(8,128)(2,1)S(1)}, u32[]{:S(2)}, u32[]{:S(2)}) collective-permute-start(bf16[3,96,128]{2,1,0:T(8,128)(2,1)S(1)} %get-tuple-element.197), channel_id=1, source_target_pairs={{0,3},{1,2},{2,1},{3,0},{4,7},{5,6},{6,5},{7,4},{8,11},{9,10},{10,... | collective-permute-start | bytes 221192 | tf_op jit(solution)/shard_map/ppermute | solution.py:29
  77.2 0.1 collective-permute-start.3
  77.3 2.5 %collective-permute-start.4 = (bf16[3,96,128]{2,1,0:T(8,128)(2,1)S(1)}, bf16[3,96,128]{2,1,0:T(8,128)(2,1)S(1)}, u32[]{:S(2)}, u32[]{:S(2)}) collective-permute-start(bf16[3,96,128]{2,1,0:T(8,128)(2,1)S(1)} %get-tuple-element.195), channel_id=1, source_target_pairs={{0,5},{1,4},{2,7},{3,6},{4,1},{5,0},{6,3},{7,2},{8,13},{9,12},{10,... | collective-permute-start | bytes 221192 | tf_op jit(solution)/shard_map/ppermute | solution.py:29
  79.8 0.9 bitcast_dynamic-update-slice_fusion.7
  80.7 0.0 collective-permute-done
  80.7 1.3 %collective-permute-start.5 = (bf16[3,96,128]{2,1,0:T(8,128)(2,1)S(1)}, bf16[3,96,128]{2,1,0:T(8,128)(2,1)S(1)}, u32[]{:S(2)}, u32[]{:S(2)}) collective-permute-start(bf16[3,96,128]{2,1,0:T(8,128)(2,1)S(1)} %get-tuple-element.194), channel_id=1, source_target_pairs={{0,6},{1,7},{2,4},{3,5},{4,2},{5,3},{6,0},{7,1},{8,14},{9,15},{10,... | collective-permute-start | bytes 221192 | tf_op jit(solution)/shard_map/ppermute | solution.py:29
  82.0 0.0 collective-permute-done.1
  82.0 2.4 %collective-permute-start.6 = (bf16[3,96,128]{2,1,0:T(8,128)(2,1)S(1)}, bf16[3,96,128]{2,1,0:T(8,128)(2,1)S(1)}, u32[]{:S(2)}, u32[]{:S(2)}) collective-permute-start(bf16[3,96,128]{2,1,0:T(8,128)(2,1)S(1)} %get-tuple-element.193), channel_id=1, source_target_pairs={{0,7},{1,6},{2,5},{3,4},{4,3},{5,2},{6,1},{7,0},{8,15},{9,14},{10,... | collective-permute-start | bytes 221192 | tf_op jit(solution)/shard_map/ppermute | solution.py:29
  84.4 0.0 collective-permute-done.2
  84.5 4.7 %collective-permute-done.3 = bf16[3,96,128]{2,1,0:T(8,128)(2,1)S(1)} collective-permute-done((bf16[3,96,128]{2,1,0:T(8,128)(2,1)S(1)}, bf16[3,96,128]{2,1,0:T(8,128)(2,1)S(1)}, u32[]{:S(2)}, u32[]{:S(2)}) %collective-permute-start.3) | collective-permute-done | bytes 73760 | tf_op jit(solution)/shard_map/ppermute | solution.py:29
  89.2 0.9 collective-permute-done.4
  90.1 0.0 collective-permute-done.5
  90.2 0.0 collective-permute-done.6
  90.2 0.7 gather_fusion
  90.9 1.0 %copy.38 = bf16[1,24,12,8,128]{4,3,1,2,0:T(8,128)(2,1)} copy(bf16[1,24,12,8,128]{4,3,2,1,0:T(8,128)(2,1)S(1)} %bitcast.132) | data formatting | bytes 1179648 | tf_op jit(solution)/shard_map/reshape | solution.py:116
  (35 shorter events, 0.3 us)
Async XLA Ops:
  0.0 42.1 %copy-start = (f32[24,128]{1,0:T(8,128)S(1)}, f32[24,128]{1,0:T(8,128)}, u32[]{:S(2)}) copy-start(f32[24,128]{1,0:T(8,128)} %param.15) | copy-start | bytes 36868
  0.0 8.6 %copy-start.1 = (bf16[1,96,3072]{2,1,0:T(8,128)(2,1)S(1)}, bf16[1,96,3072]{2,1,0:T(8,128)(2,1)}, u32[]{:S(2)}) copy-start(bf16[1,96,3072]{2,1,0:T(8,128)(2,1)} %param.12) | copy-start | bytes 1769476
  2.1 27.4 %copy-start.4 = (u32[32]{0:T(128)S(1)}, u32[32]{0:T(128)}, u32[]{:S(2)}) copy-start(u32[32]{0:T(128)} %constant.115) | copy-start | bytes 388
  2.1 28.7 %copy-start.3 = (s32[24]{0:T(128)S(1)}, s32[24]{0:T(128)}, u32[]{:S(2)}) copy-start(s32[24]{0:T(128)} %param.14) | copy-start | bytes 292
  2.2 38.9 %copy-start.2 = (bf16[1,96,3072]{2,1,0:T(8,128)(2,1)S(1)}, bf16[1,96,3072]{2,1,0:T(8,128)(2,1)}, u32[]{:S(2)}) copy-start(bf16[1,96,3072]{2,1,0:T(8,128)(2,1)} %param.10) | copy-start | bytes 1769476
  2.2 23.2 %all-to-all-start.1 = ((bf16[24,96,128]{2,1,0:T(8,128)(2,1)}), bf16[24,96,128]{2,1,0:T(8,128)(2,1)S(1)}, u32[]{:S(2)}, u32[]{:S(2)}) async-start(bf16[24,96,128]{2,1,0:T(8,128)(2,1)} %copy.23), calls=%async_computation.1 | async-start | bytes 1179648 | tf_op jit(solution)/shard_map/all_to_all | solution.py:91
  25.4 20.2 %all-to-all-start.2 = ((bf16[24,96,128]{2,1,0:T(8,128)(2,1)}), bf16[24,96,128]{2,1,0:T(8,128)(2,1)S(1)}, u32[]{:S(2)}, u32[]{:S(2)}) async-start(bf16[24,96,128]{2,1,0:T(8,128)(2,1)} %copy.25), calls=%async_computation.2 | async-start | bytes 1179648 | tf_op jit(solution)/shard_map/all_to_all | solution.py:92
  45.6 20.2 %all-to-all-start = ((bf16[24,96,128]{2,1,0:T(8,128)(2,1)}), bf16[24,96,128]{2,1,0:T(8,128)(2,1)S(1)}, u32[]{:S(2)}, u32[]{:S(2)}) async-start(bf16[24,96,128]{2,1,0:T(8,128)(2,1)} %copy.21), calls=%async_computation | async-start | bytes 1179648 | tf_op jit(solution)/shard_map/all_to_all | solution.py:90
  75.3 5.4 %collective-permute-start = (bf16[3,96,128]{2,1,0:T(8,128)(2,1)S(1)}, bf16[3,96,128]{2,1,0:T(8,128)(2,1)S(1)}, u32[]{:S(2)}, u32[]{:S(2)}) collective-permute-start(bf16[3,96,128]{2,1,0:T(8,128)(2,1)S(1)} %get-tuple-element.199), channel_id=1, source_target_pairs={{0,1},{1,0},{2,3},{3,2},{4,5},{5,4},{6,7},{7,6},{8,9},{9,8},{10,11... | collective-permute-start | bytes 221192 | tf_op jit(solution)/shard_map/ppermute | solution.py:29
  75.3 6.7 %collective-permute-start.1 = (bf16[3,96,128]{2,1,0:T(8,128)(2,1)S(1)}, bf16[3,96,128]{2,1,0:T(8,128)(2,1)S(1)}, u32[]{:S(2)}, u32[]{:S(2)}) collective-permute-start(bf16[3,96,128]{2,1,0:T(8,128)(2,1)S(1)} %get-tuple-element.198), channel_id=1, source_target_pairs={{0,2},{1,3},{2,0},{3,1},{4,6},{5,7},{6,4},{7,5},{8,10},{9,11},{10,... | collective-permute-start | bytes 221192 | tf_op jit(solution)/shard_map/ppermute | solution.py:29
  75.4 9.0 %collective-permute-start.2 = (bf16[3,96,128]{2,1,0:T(8,128)(2,1)S(1)}, bf16[3,96,128]{2,1,0:T(8,128)(2,1)S(1)}, u32[]{:S(2)}, u32[]{:S(2)}) collective-permute-start(bf16[3,96,128]{2,1,0:T(8,128)(2,1)S(1)} %get-tuple-element.197), channel_id=1, source_target_pairs={{0,3},{1,2},{2,1},{3,0},{4,7},{5,6},{6,5},{7,4},{8,11},{9,10},{10,... | collective-permute-start | bytes 221192 | tf_op jit(solution)/shard_map/ppermute | solution.py:29
  77.2 12.0 %collective-permute-start.3 = (bf16[3,96,128]{2,1,0:T(8,128)(2,1)S(1)}, bf16[3,96,128]{2,1,0:T(8,128)(2,1)S(1)}, u32[]{:S(2)}, u32[]{:S(2)}) collective-permute-start(bf16[3,96,128]{2,1,0:T(8,128)(2,1)S(1)} %get-tuple-element.196), channel_id=1, source_target_pairs={{0,4},{1,5},{2,6},{3,7},{4,0},{5,1},{6,2},{7,3},{8,12},{9,13},{10,... | collective-permute-start | bytes 221192 | tf_op jit(solution)/shard_map/ppermute | solution.py:29
  77.3 12.8 %collective-permute-start.4 = (bf16[3,96,128]{2,1,0:T(8,128)(2,1)S(1)}, bf16[3,96,128]{2,1,0:T(8,128)(2,1)S(1)}, u32[]{:S(2)}, u32[]{:S(2)}) collective-permute-start(bf16[3,96,128]{2,1,0:T(8,128)(2,1)S(1)} %get-tuple-element.195), channel_id=1, source_target_pairs={{0,5},{1,4},{2,7},{3,6},{4,1},{5,0},{6,3},{7,2},{8,13},{9,12},{10,... | collective-permute-start | bytes 221192 | tf_op jit(solution)/shard_map/ppermute | solution.py:29
  80.7 9.4 %collective-permute-start.5 = (bf16[3,96,128]{2,1,0:T(8,128)(2,1)S(1)}, bf16[3,96,128]{2,1,0:T(8,128)(2,1)S(1)}, u32[]{:S(2)}, u32[]{:S(2)}) collective-permute-start(bf16[3,96,128]{2,1,0:T(8,128)(2,1)S(1)} %get-tuple-element.194), channel_id=1, source_target_pairs={{0,6},{1,7},{2,4},{3,5},{4,2},{5,3},{6,0},{7,1},{8,14},{9,15},{10,... | collective-permute-start | bytes 221192 | tf_op jit(solution)/shard_map/ppermute | solution.py:29
  82.0 8.1 %collective-permute-start.6 = (bf16[3,96,128]{2,1,0:T(8,128)(2,1)S(1)}, bf16[3,96,128]{2,1,0:T(8,128)(2,1)S(1)}, u32[]{:S(2)}, u32[]{:S(2)}) collective-permute-start(bf16[3,96,128]{2,1,0:T(8,128)(2,1)S(1)} %get-tuple-element.193), channel_id=1, source_target_pairs={{0,7},{1,6},{2,5},{3,4},{4,3},{5,2},{6,1},{7,0},{8,15},{9,14},{10,... | collective-permute-start | bytes 221192 | tf_op jit(solution)/shard_map/ppermute | solution.py:29
